TPU v7x, 512 devices: a whole 4x8x8 slice. The times are simulated.
512 devices in a mesh: inner: 32 (over z_lo, y, core), outer: 16 (over x, z_hi).
Axes of the slice: x: 4, y: 8, z: 8 (z_hi: 4, z_lo: 2; z = z_hi * 2 + z_lo), core: 2. Of those that a mesh axis runs over, the one named last changes fastest.
Arguments:
- gradients: bfloat16 [32, 16, 256, 8192], P('inner', 'outer'), may hold values from -6 to 6
- master_shard: float32 [256, 8192], P('outer', 'inner'), may hold values from -6 to 6
- first_moment: float32 [256, 8192], P('outer', 'inner'), may hold values from -48 to 48
- second_moment: float32 [256, 8192], P('outer', 'inner'), may hold values from 100 to 1000
Outputs:
- new_master: float32 [256, 8192], P('outer', 'inner')
- new_first: float32 [256, 8192], P('outer', 'inner')
- new_second: float32 [256, 8192], P('outer', 'inner')
- group_weights: bfloat16 [256, 8192], P(None, 'inner')
All inputs are finite; a program needn't handle non-finite values.
Results may differ from a plain program's by a relative error of at most 0.0025.
Values may be sent and summed in bfloat16 or wider, within the bound.
A program may use at most 64 MiB of HBM per device.

v0:
```python
import jax
import jax.numpy as jnp
from jax import lax
from jax.sharding import PartitionSpec as P

beta_first = 0.9
beta_second = 0.95
learn_rate = 0.05
decay_rate = 0.1
adam_eps = 1e-05
bias_first = 1.0 - 0.9**10
bias_second = 1.0 - 0.95**10


def sum_sources(pieces):
    return jnp.sum(pieces.astype(jnp.float32), axis=0)


def body(gradients, master_shard, first_moment, second_moment):
    local = gradients.reshape(1, gradients.shape[2], gradients.shape[3])
    partial_value = sum_sources(
        lax.all_to_all(local, "inner", split_axis=2, concat_axis=0, tiled=True)
    )
    reduced = sum_sources(
        lax.all_to_all(
            partial_value[None].astype(jnp.bfloat16),
            "outer",
            split_axis=1,
            concat_axis=0,
            tiled=True,
        ).astype(jnp.float32)
    )
    new_first = beta_first * first_moment + (1.0 - beta_first) * reduced
    new_second = beta_second * second_moment + (1.0 - beta_second) * reduced * reduced
    update = (
        new_first / bias_first / (jnp.sqrt(new_second / bias_second) + adam_eps)
        + decay_rate * master_shard
    )
    new_master = master_shard - learn_rate * update
    copy_weights = lax.all_gather(new_master.astype(jnp.bfloat16), "outer", axis=0, tiled=True)
    return (new_master, new_first, new_second, copy_weights)


def solution(mesh):
    return jax.shard_map(
        body,
        mesh=mesh,
        in_specs=(
            P("inner", "outer", None, None),
            P("outer", "inner"),
            P("outer", "inner"),
            P("outer", "inner"),
        ),
        out_specs=(P("outer", "inner"), P("outer", "inner"), P("outer", "inner"), P(None, "inner")),
        check_vma=False,
    )
```

profile of v0, /device:TPU:8, one launch (start us, length us, event | category | flops | bytes accessed | tf_op | source)
XLA Modules:
  0.0 269.7 jit_solution(8920335155351503580)
XLA Ops:
  0.6 17.9 %copy.11 = bf16[1,256,8192]{1,0,2:T(2,128)(2,1)} copy(bf16[1,256,8192]{2,1,0:T(8,128)(2,1)} %bitcast.11) | data formatting | bytes 8388608 | tf_op jit(solution)/shard_map/reshape | solution.py:20
  18.5 0.5 broadcast.18
  19.0 43.5 %reduce.4 = bf16[8192,256]{1,0:T(8,128)(2,1)} reduce(bf16[8192,1,256]{2,1,0:T(2,128)(2,1)} %bitcast.8, bf16[]{:T(256)} %broadcast.18), dimensions={1}, to_apply=%bitcast.4.reduce_sub_computation | reduce | bytes 8388610
  62.5 6.9 %reshape.29 = bf16[32,2,32768]{2,1,0:T(2,128)(2,1)} reshape(bf16[8192,256]{1,0:T(8,128)(2,1)} %reduce.4) | data formatting | bytes 8388608
  69.4 106.8 %all_to_all.21 = bf16[32,2,32768]{2,1,0:T(2,128)(2,1)} all-to-all(bf16[32,2,32768]{2,1,0:T(2,128)(2,1)} %reshape.29), channel_id=1, replica_groups=mesh['inner'=32,'outer'=16] {'inner'}, dimensions={0} | all-to-all | bytes 8388608 | tf_op jit(solution)/shard_map/all_to_all | solution.py:22
  176.2 19.8 %reshape.30 = bf16[8192,1,256]{2,1,0:T(2,128)(2,1)} reshape(bf16[32,2,32768]{2,1,0:T(2,128)(2,1)} %all_to_all.21) | data formatting | bytes 8388608
  196.0 6.1 %copy.16 = bf16[1,256,8192]{1,2,0:T(8,128)(2,1)} copy(bf16[1,256,8192]{1,0,2:T(2,128)(2,1)} %bitcast.9) | data formatting | bytes 8388608
  202.1 0.0 copy-start
  202.1 0.0 copy-start.1
  202.1 0.0 copy-start.2
  202.1 2.8 %reduce_sum.21 = bf16[256,256]{0,1:T(8,128)(2,1)S(1)} reduce(bf16[256,32,256]{0,2,1:T(8,128)(2,1)} %bitcast.10, bf16[]{:T(256)} %constant.4.clone.1), dimensions={1}, to_apply=%region_0.0 | reduce | flops 2031616 | bytes 4325378 | tf_op jit(solution)/shard_map/reduce_sum | solution.py:16
  204.9 0.2 copy.13
  205.1 1.4 reduce.5
  206.6 21.7 %all_to_all.22 = bf16[16,2,2048]{2,1,0:T(2,128)(2,1)S(1)} all-to-all(bf16[16,2,2048]{2,1,0:T(2,128)(2,1)S(1)} %reshape.31), channel_id=1, replica_groups=mesh['inner'=32,'outer'=16] {'outer'}, dimensions={0} | all-to-all | bytes 262144 | tf_op jit(solution)/shard_map/all_to_all | solution.py:25
  228.3 0.1 reshape.32
  228.5 0.0 copy-done
  228.5 0.0 copy-done.1
  228.5 0.0 copy-done.2
  228.5 0.6 fusion.1
  229.1 39.9 %all_gather.3 = bf16[256,256]{1,0:T(8,128)(2,1)S(1)} all-gather(bf16[16,256]{1,0:T(8,128)(2,1)S(1)} %get-tuple-element.4), channel_id=1, replica_groups=mesh['inner'=32,'outer'=16] {'outer'}, dimensions={0}, use_global_device_ids=true | all-gather | bytes 139264 | tf_op jit(solution)/shard_map/all_gather | solution.py:40
  269.0 0.7 copy.19
  (3 shorter events, 0.1 us)
Async XLA Ops:
  202.1 26.4 %copy-start = (f32[16,256]{1,0:T(8,128)S(1)}, f32[16,256]{1,0:T(8,128)}, u32[]{:S(2)}) copy-start(f32[16,256]{1,0:T(8,128)} %param.5) | copy-start | bytes 49156
  202.1 26.4 %copy-start.1 = (f32[16,256]{1,0:T(8,128)S(1)}, f32[16,256]{1,0:T(8,128)}, u32[]{:S(2)}) copy-start(f32[16,256]{1,0:T(8,128)} %param.6) | copy-start | bytes 49156
  202.1 26.4 %copy-start.2 = (f32[16,256]{1,0:T(8,128)S(1)}, f32[16,256]{1,0:T(8,128)}, u32[]{:S(2)}) copy-start(f32[16,256]{1,0:T(8,128)} %param.7) | copy-start | bytes 49156
where the time goes:
time: 271 us; the launch traced here: 270 us
  blocking collectives  168 us (62%)
  local copies, waits for them, and re-layouts  52.1 us (19%)
  other arithmetic  48.4 us (18%)
    all_to_all x1, blocking collectives, body(): lax.all_to_all(local, 'inner', split_axis=2, concat_axis=0, tiled=True)  107 us
    unnamed x2, other arithmetic  44.9 us
    all_gather x1, blocking collectives, body(): lax.all_gather(new_master.astype(jnp.bfloat16), 'outer', axis=0, tiled=True)  39.9 us
    unnamed x14, local copies, waits for them, and re-layouts  34.1 us
    all_to_all x1, blocking collectives, body(): lax.all_to_all(partial_value[None].astype(jnp.bfloat16), 'outer', split_a...  21.7 us
    reshape x1, local copies, waits for them, and re-layouts, body(): local = gradients.reshape(1, gradients.shape[2], gradients.shape[3])  17.9 us

commit v1 on v0

v1 whole, which is shorter than its diff:
```python
import jax
import jax.numpy as jnp
from jax import lax
from jax.experimental import pallas as pl
from jax.experimental.pallas import tpu as pltpu
from jax.sharding import PartitionSpec as P

MESH = pl.DeviceIdType.MESH
F32 = jnp.float32
BF16 = jnp.bfloat16

beta_first = 0.9
beta_second = 0.95
learn_rate = 0.05
decay_rate = 0.1
adam_eps = 1e-05
bias_first = 1.0 - 0.9**10
bias_second = 1.0 - 0.95**10

NX, NY, NZ = 4, 8, 8


def device(x, y, z, core):
    return ((z % 2) * 16 + y * 2 + core, x * 4 + z // 2)


def adam(total, master, first, second):
    new_first = beta_first * first + (1.0 - beta_first) * total
    new_second = beta_second * second + (1.0 - beta_second) * total * total
    update = (
        new_first / bias_first / (jnp.sqrt(new_second / bias_second) + adam_eps)
        + decay_rate * master
    )
    return master - learn_rate * update, new_first, new_second


def kernel(
    grad, master_in, first_in, second_in,
    master_out, first_out, second_out, weights_out,
    own, other, sent_a, got_a, sent_y, got_y, sent_z, got_z,
    part_a, got_a2, sum_a, got_a3,
    part_y, part_z, got_h2, sum_h, got_h3,
    state, result, weights,
    load_sem, state_sem, store_sem,
    core_s, core_r, a_s, a_r, y_s, y_r, z_s, z_r,
    a2_s, a2_r, h2_s, h2_r, a3_s, a3_r, h3_s, h3_r, w_s, w_r,
):
    inner = lax.axis_index("inner")
    outer = lax.axis_index("outer")
    core = inner % 2
    y = (inner // 2) % NY
    x = outer // 4
    z_hi = outer % 4
    z_lo = inner // 16
    z = z_hi * 2 + z_lo
    odd = (y + z) % 2

    def at_x(d):
        return device((x + d) % NX, y, z, core)

    def at_y(d):
        return device(x, (y + d) % NY, z, core)

    def at_z(d):
        return device(x, y, (z + d) % NZ, core)

    def remote(src, dst, send, recv, target):
        return pltpu.make_async_remote_copy(
            src_ref=src, dst_ref=dst, send_sem=send, recv_sem=recv,
            device_id=target, device_id_type=MESH,
        )

    barrier = pltpu.get_barrier_semaphore()
    peers = (
        [device(x, y, z, 1 - core)]
        + [at_x(d) for d in range(1, NX)]
        + [at_y(d) for d in range(1, NY)]
        + [at_z(d) for d in range(1, NZ)]
    )
    for peer in peers:
        pl.semaphore_signal(barrier, inc=1, device_id=peer, device_id_type=MESH)

    def column(p, i, which):
        cy = (y + 1 + i) % NY
        start = (((cy + p) % 2) * 16 + cy * 2 + which) * 256
        return pl.ds(pl.multiple_of(start, 256), 256)

    def load(p, i):
        return pltpu.make_async_copy(
            grad.at[:, column(p, i, core)], own.at[p, i], load_sem.at[p, i]
        )

    def swap(p, i):
        return remote(
            grad.at[:, column(p, i, 1 - core)], other.at[p, i],
            core_s.at[p, i], core_r.at[p, i], device(x, y, z, 1 - core),
        )

    def each(count, step):
        def body(i, carry):
            step(i)
            return carry

        lax.fori_loop(0, count, body, 0)

    for p in range(2):
        each(NY, lambda i: load(p, i).start())
    states = [
        pltpu.make_async_copy(ref, state.at[n], state_sem.at[n])
        for n, ref in enumerate((master_in, first_in, second_in))
    ]
    for copy in states:
        copy.start()

    pl.semaphore_wait(barrier, len(peers))
    for p in range(2):
        each(NY, lambda i: swap(p, i).start())

    def send_a(p, k):
        return remote(
            sent_a.at[p, k], got_a.at[p, k - 1],
            a_s.at[p, k - 1], a_r.at[p, k - 1], at_x(k),
        )

    def send_y(p, d):
        return remote(
            sent_y.at[(y + d) % NY, p], got_y.at[d - 1, p],
            y_s.at[p, d - 1], y_r.at[p, d - 1], at_y(d),
        )

    def send_z(p, d):
        return remote(
            sent_z.at[(z + d) % NZ, p], got_z.at[d - 1, p],
            z_s.at[p, d - 1], z_r.at[p, d - 1], at_z(d),
        )

    for p in range(2):

        def chip_sum(i):
            load(p, i).wait()
            swap(p, i).wait_recv()
            cy = (y + 1 + i) % NY
            cz = (cy + p) % 2
            for k in range(NX):
                rows = pl.ds(pl.multiple_of(((x + k) % NX) * 64, 64), 64)
                value = (
                    own[p, i, rows, :].astype(F32) + other[p, i, rows, :].astype(F32)
                ).astype(BF16)
                sent_a[p, k, cy] = value[:, :128]
                if k % 2 == 1:
                    sent_y[cy, p, k // 2] = value[:, 128:]
                else:
                    for hi in range(4):
                        sent_z[hi * 2 + cz, p, cy // 2, k // 2] = value[
                            hi * 16 : hi * 16 + 16, 128:
                        ]

            @pl.when(i < NY - 1)
            def _():
                send_y(p, i + 1).start()

        each(NY, chip_sum)
        for k in range(1, NX):
            send_a(p, k).start()
        each(NZ - 1, lambda i: send_z(p, i + 1).start())

    def send_a2(p, d):
        if p == 0:
            src, target = part_a.at[p, (y + d) % NY], at_y(d)
        else:
            src, target = part_a.at[p, (z + d) % NZ], at_z(d)
        return remote(
            src, got_a2.at[p, d - 1], a2_s.at[p, d - 1], a2_r.at[p, d - 1], target
        )

    for p in range(2):
        for k in range(1, NX):
            send_a(p, k).wait_recv()

        def x_sum(cy):
            value = sent_a[p, 0, cy].astype(F32)
            for k in range(NX - 1):
                value += got_a[p, k, cy].astype(F32)
            value = value.astype(BF16)
            for hi in range(4):
                if p == 0:
                    part_a[p, cy, hi] = value[hi * 16 : hi * 16 + 16]
                else:
                    part_a[p, hi * 2 + (cy + 1) % 2, cy // 2] = value[hi * 16 : hi * 16 + 16]

        each(NY, x_sum)
        each(NY - 1, lambda i: send_a2(p, i + 1).start())

    def send_h2(way, d):
        if way == 0:
            src, target = part_y.at[(z + d) % NZ], at_z(d)
        else:
            src, target = part_z.at[(y + d) % NY], at_y(d)
        return remote(
            src, got_h2.at[way, d - 1], h2_s.at[way, d - 1], h2_r.at[way, d - 1], target
        )

    for p in range(2):
        each(NY - 1, lambda i: send_y(p, i + 1).wait_recv())
        for k in range(2):
            value = sent_y[y, p, k].astype(F32)
            for d in range(NY - 1):
                value += got_y[d, p, k].astype(F32)
            value = value.astype(BF16)
            for hi in range(4):
                part_y[hi * 2 + (y + p) % 2, k] = value[hi * 16 : hi * 16 + 16]
    each(NZ - 1, lambda i: send_h2(0, i + 1).start())

    for p in range(2):
        each(NZ - 1, lambda i: send_z(p, i + 1).wait_recv())

        def z_sum(ci):
            for k in range(2):
                value = sent_z[z, p, ci, k].astype(F32)
                for d in range(NZ - 1):
                    value += got_z[d, p, ci, k].astype(F32)
                part_z[2 * ci + (z + p) % 2, k] = value.astype(BF16)

        each(4, z_sum)
    each(NY - 1, lambda i: send_h2(1, i + 1).start())

    def send_a3(d):
        along_z = (odd + d + 1) % 2
        to_y = (y + (1 - along_z) * d) % NY
        to_z = (z + along_z * d) % NZ
        index = (along_z * to_z + (1 - along_z) * to_y) // 2
        return remote(
            sum_a.at[1 - along_z, index], got_a3.at[d - 1],
            a3_s.at[d - 1], a3_r.at[d - 1], device(x, to_y, to_z, core),
        )

    for p in range(2):
        each(NY - 1, lambda i: send_a2(p, i + 1).wait_recv())
        for n in range(4):
            value = part_a[p, y if p == 0 else z, n].astype(F32)
            for d in range(NY - 1):
                value += got_a2[p, d, n].astype(F32)
            sum_a[p, n] = value.astype(BF16)
    each(NY - 1, lambda i: send_a3(i + 1).start())

    def send_h3(k):
        return remote(
            sum_h.at[k], got_h3.at[k - 1], h3_s.at[k - 1], h3_r.at[k - 1], at_x(k)
        )

    for way in range(2):
        each(NZ - 1, lambda i: send_h2(way, i + 1).wait_recv())
        for k in range(2):
            value = (part_y[z, k] if way == 0 else part_z[y, k]).astype(F32)
            for d in range(NZ - 1):
                value += got_h2[way, d, k].astype(F32)
            sum_h[2 * k + 1 - way] = value.astype(BF16)
    for k in range(1, NX):
        send_h3(k).start()

    for copy in states:
        copy.wait()

    def finish(half, total):
        cols = slice(half * 128, half * 128 + 128)
        new_master, new_first, new_second = adam(
            total, state[0, :, cols], state[1, :, cols], state[2, :, cols]
        )
        result[0, :, cols] = new_master
        result[1, :, cols] = new_first
        result[2, :, cols] = new_second
        weights[:, cols] = new_master.astype(BF16)

    for k in range(1, NX):
        send_h3(k).wait_recv()
    total = sum_h[0].astype(F32)
    for k in range(NX - 1):
        total += got_h3[k].astype(F32)
    finish(1, total)

    each(NY - 1, lambda i: send_a3(i + 1).wait_recv())
    last = (z * (1 - odd) + y * odd) // 2
    total = sum_a[odd, last].astype(F32)
    for d in range(NY - 1):
        total += got_a3[d].astype(F32)
    finish(0, total)

    rows = pl.ds(pl.multiple_of(outer * 16, 16), 16)

    def spread(n):
        return remote(
            weights, weights_out.at[rows], w_s.at[n - 1], w_r.at[n - 1],
            (inner, ((x + n // 4) % 4) * 4 + (z_hi + n % 4) % 4),
        )

    def arrive(n):
        source = ((x - n // 4 + 4) % 4) * 4 + (z_hi - n % 4 + 4) % 4
        return remote(
            weights, weights_out.at[pl.ds(pl.multiple_of(source * 16, 16), 16)],
            w_s.at[n - 1], w_r.at[n - 1], (inner, source),
        )

    each(15, lambda i: spread(i + 1).start())
    stores = [
        pltpu.make_async_copy(result.at[n], ref, store_sem.at[n])
        for n, ref in enumerate((master_out, first_out, second_out))
    ] + [pltpu.make_async_copy(weights, weights_out.at[rows], store_sem.at[3])]
    for copy in stores:
        copy.start()

    for p in range(2):
        each(NY, lambda i: swap(p, i).wait_send())
        for k in range(1, NX):
            send_a(p, k).wait_send()
        each(NY - 1, lambda i: send_y(p, i + 1).wait_send())
        each(NY - 1, lambda i: send_z(p, i + 1).wait_send())
        each(NY - 1, lambda i: send_a2(p, i + 1).wait_send())
        each(NY - 1, lambda i: send_h2(p, i + 1).wait_send())
    each(NY - 1, lambda i: send_a3(i + 1).wait_send())
    for k in range(1, NX):
        send_h3(k).wait_send()
    for copy in stores:
        copy.wait()
    each(15, lambda i: spread(i + 1).wait_send())
    each(15, lambda i: arrive(i + 1).wait_recv())


def body(gradients, master_shard, first_moment, second_moment):
    grad = gradients.reshape(gradients.shape[2], gradients.shape[3])
    hbm = pl.BlockSpec(memory_space=pltpu.HBM)
    dma = pltpu.SemaphoreType.DMA
    shard = jax.ShapeDtypeStruct(master_shard.shape, F32)
    return pl.pallas_call(
        kernel,
        out_shape=(shard, shard, shard, jax.ShapeDtypeStruct((256, 256), BF16)),
        in_specs=[hbm] * 4,
        out_specs=(hbm,) * 4,
        scratch_shapes=[
            pltpu.VMEM((2, 8, 256, 256), BF16),
            pltpu.VMEM((2, 8, 256, 256), BF16),
            pltpu.VMEM((2, 4, 8, 64, 128), BF16),
            pltpu.VMEM((2, 3, 8, 64, 128), BF16),
            pltpu.VMEM((8, 2, 2, 64, 128), BF16),
            pltpu.VMEM((7, 2, 2, 64, 128), BF16),
            pltpu.VMEM((8, 2, 4, 2, 16, 128), BF16),
            pltpu.VMEM((7, 2, 4, 2, 16, 128), BF16),
            pltpu.VMEM((2, 8, 4, 16, 128), BF16),
            pltpu.VMEM((2, 7, 4, 16, 128), BF16),
            pltpu.VMEM((2, 4, 16, 128), BF16),
            pltpu.VMEM((7, 16, 128), BF16),
            pltpu.VMEM((8, 2, 16, 128), BF16),
            pltpu.VMEM((8, 2, 16, 128), BF16),
            pltpu.VMEM((2, 7, 2, 16, 128), BF16),
            pltpu.VMEM((4, 16, 128), BF16),
            pltpu.VMEM((3, 16, 128), BF16),
            pltpu.VMEM((3, 16, 256), F32),
            pltpu.VMEM((3, 16, 256), F32),
            pltpu.VMEM((16, 256), BF16),
            dma((2, 8)), dma((3,)), dma((4,)),
            dma((2, 8)), dma((2, 8)),
            dma((2, 3)), dma((2, 3)),
            dma((2, 7)), dma((2, 7)),
            dma((2, 7)), dma((2, 7)),
            dma((2, 7)), dma((2, 7)),
            dma((2, 7)), dma((2, 7)),
            dma((7,)), dma((7,)),
            dma((3,)), dma((3,)),
            dma((15,)), dma((15,)),
        ],
        compiler_params=pltpu.CompilerParams(
            collective_id=0, has_side_effects=True, vmem_limit_bytes=63 << 20
        ),
        name="reduce_adam_gather",
    )(grad, master_shard, first_moment, second_moment)


def solution(mesh):
    return jax.shard_map(
        body,
        mesh=mesh,
        in_specs=(
            P("inner", "outer", None, None),
            P("outer", "inner"),
            P("outer", "inner"),
            P("outer", "inner"),
        ),
        out_specs=(P("outer", "inner"), P("outer", "inner"), P("outer", "inner"), P(None, "inner")),
        check_vma=False,
    )
```

time: 271 us -> 57.2 us (0.21)
  blocking collectives: 168 us -> 0 us
  Pallas kernels: 0 us -> 50.6 us
  other arithmetic: 48.4 us -> 0 us
  local copies, waits for them, and re-layouts: 52.1 us -> 5.54 us
    all_to_all x2 -> x0, blocking collectives: 129 us -> none  [the longest x1 107 us: body(): lax.all_to_all(local, 'inner', split_axis=2, concat_axis=0, tiled=True)]
    pallas_call x0 -> x1, Pallas kernels: none -> 50.6 us  [body(): pl.pallas_call(kernel, out_shape=(shard, shard, shard, jax.ShapeDtypeStru...]
    unnamed x2 -> x0, other arithmetic: 44.9 us -> none
    all_gather x1 -> x0, blocking collectives: 39.9 us -> none  [body(): lax.all_gather(new_master.astype(jnp.bfloat16), 'outer', axis=0, tiled=True)]
    unnamed x14 -> x4, local copies, waits for them, and re-layouts: 34.1 us -> 5.54 us
    reshape x1 -> x0, local copies, waits for them, and re-layouts: 17.9 us -> none  [body(): local = gradients.reshape(1, gradients.shape[2], gradients.shape[3])]
    reduce_sum x2 -> x0, other arithmetic: 2.84 us -> none  [sum_sources(): return jnp.sum(pieces.astype(jnp.float32), axis=0)]
where the time goes in v1:
time: 57.2 us; the launch traced here: 56.8 us
  Pallas kernels  50.6 us (88%)
  local copies, waits for them, and re-layouts  5.54 us (10%)
  between operations  0.64 us (1%)
    pallas_call x1, Pallas kernels, body(): pl.pallas_call(kernel, out_shape=(shard, shard, shard, jax.ShapeDtypeStru...  50.6 us
    unnamed x4, local copies, waits for them, and re-layouts  5.54 us

profile of v1, /device:TPU:8, one launch (start us, length us, event | category | flops | bytes accessed | tf_op | source)
XLA Modules:
  0.0 56.8 jit_solution(784912224520909702)
XLA Ops:
  0.6 50.6 %reduce_adam_gather.1 = (f32[16,256]{1,0:T(8,128)}, f32[16,256]{1,0:T(8,128)}, f32[16,256]{1,0:T(8,128)}, bf16[256,256]{1,0:T(8,128)(2,1)}) custom-call(bf16[256,8192]{1,0:T(8,128)(2,1)} %bitcast.1, f32[16,256]{1,0:T(8,128)} %master_in.1, f32[16,256]{1,0:T(8,128)} %first_in.1, f32[16,256]{1,0:T(8,128)} %second_in.1), custom_call_target="tpu_custom_call" | custom-call | tf_op jit(solution)/shard_map/reduce_adam_gather/pallas_call | solution.py:333
  51.3 1.3 %copy.12 = f32[16,256]{1,0:T(8,128)} copy(f32[16,256]{1,0:T(8,128)} %get-tuple-element.8) | data formatting | bytes 32768
  52.6 1.3 %copy.13 = f32[16,256]{1,0:T(8,128)} copy(f32[16,256]{1,0:T(8,128)} %get-tuple-element.9) | data formatting | bytes 32768
  53.9 1.3 %copy.14 = f32[16,256]{1,0:T(8,128)} copy(f32[16,256]{1,0:T(8,128)} %get-tuple-element.10) | data formatting | bytes 32768
  55.2 1.6 %copy.15 = bf16[256,256]{1,0:T(8,128)(2,1)} copy(bf16[256,256]{1,0:T(8,128)(2,1)} %get-tuple-element.11) | data formatting | bytes 262144

commit v2 on v1

v2 whole, which is shorter than its diff:
```python
import jax
import jax.numpy as jnp
from jax import lax
from jax.experimental import pallas as pl
from jax.experimental.pallas import tpu as pltpu
from jax.sharding import PartitionSpec as P

MESH = pl.DeviceIdType.MESH
F32 = jnp.float32
BF16 = jnp.bfloat16

beta_first = 0.9
beta_second = 0.95
learn_rate = 0.05
decay_rate = 0.1
adam_eps = 1e-05
bias_first = 1.0 - 0.9**10
bias_second = 1.0 - 0.95**10

NX, NY, NZ = 4, 8, 8


def device(x, y, z, core):
    return ((z % 2) * 16 + y * 2 + core, x * 4 + z // 2)


def adam(total, master, first, second):
    new_first = beta_first * first + (1.0 - beta_first) * total
    new_second = beta_second * second + (1.0 - beta_second) * total * total
    update = (
        new_first / bias_first / (jnp.sqrt(new_second / bias_second) + adam_eps)
        + decay_rate * master
    )
    return master - learn_rate * update, new_first, new_second


def each(count, step, first=0):
    def body(i, carry):
        step(i)
        return carry

    lax.fori_loop(first, count, body, 0)


def distance(i):
    return (((i // 2 + 1) * (1 - 2 * (i % 2)) + 8) % 8) * (1 - i // 7)


def hops(n):
    return min(n // 4, 4 - n // 4) + 2 * min(n % 4, 4 - n % 4)


def kernel(
    grad, master_in, first_in, second_in,
    state_out, weights_out,
    own, other, sent_a, got_a, sent_y, got_y, sent_z, got_z,
    part_a, got_a2, sum_a, got_a3, part_h, got_h2, sum_h, got_h3,
    state, result, weights,
    load_sem, state_sem, store_sem, far_sem,
    core_s, core_r, a_s, a_r, y_s, y_r, z_s, z_r,
    a2_s, a2_r, h2_s, h2_r, a3_s, a3_r, h3_s, h3_r, w_s, w_r,
):
    inner = lax.axis_index("inner")
    outer = lax.axis_index("outer")
    core = inner % 2
    y = (inner // 2) % NY
    x = outer // 4
    z_hi = outer % 4
    z = z_hi * 2 + inner // 16
    odd = (y + z) % 2

    def at_x(d):
        return device((x + d) % NX, y, z, core)

    def at_y(d):
        return device(x, (y + d) % NY, z, core)

    def at_z(d):
        return device(x, y, (z + d) % NZ, core)

    sibling = device(x, y, z, 1 - core)

    def remote(src, dst, send, recv, target):
        return pltpu.make_async_remote_copy(
            src_ref=src, dst_ref=dst, send_sem=send, recv_sem=recv,
            device_id=target, device_id_type=MESH,
        )

    barrier = pltpu.get_barrier_semaphore()
    near = (
        [at_x(d) for d in (2, 1, 3)]
        + [at_y(d) for d in (2, 6, 1, 7)]
        + [at_z(d) for d in (2, 6, 1, 7)]
        + [sibling]
    )
    for peer in near:
        pl.semaphore_signal(barrier, inc=1, device_id=peer, device_id_type=MESH)

    def column(p, i, which):
        cy = (y + distance(i)) % NY
        start = (((cy + p) % 2) * 16 + cy * 2 + which) * 256
        return pl.ds(pl.multiple_of(start, 256), 256)

    def load(p, i):
        return pltpu.make_async_copy(
            grad.at[:, column(p, i, core)], own.at[p, i], load_sem.at[p, i]
        )

    def swap(p, i):
        return remote(
            grad.at[:, column(p, i, 1 - core)], other.at[p, i],
            core_s.at[p, i], core_r.at[p, i], sibling,
        )

    for p in range(2):
        each(NY, lambda i: load(p, i).start())
    states = [
        pltpu.make_async_copy(ref, state.at[n], state_sem.at[n])
        for n, ref in enumerate((master_in, first_in, second_in))
    ]
    for copy in states:
        copy.start()

    pl.semaphore_wait(barrier, len(near))
    two_away = (at_y(2), at_y(6), at_z(2), at_z(6))
    for n, peer in enumerate(two_away):
        pl.semaphore_signal(far_sem.at[n], inc=1, device_id=peer, device_id_type=MESH)
    for p in range(2):
        each(NY, lambda i: swap(p, i).start())

    def send_a(p, part, k):
        blocks = pl.ds(part * 4, 4)
        return remote(
            sent_a.at[p, k, blocks], got_a.at[p, k - 1, blocks],
            a_s.at[p, part, k - 1], a_r.at[p, part, k - 1], at_x(k),
        )

    def send_y(p, d):
        return remote(
            sent_y.at[(y + d) % NY, p], got_y.at[d - 1, p],
            y_s.at[p, d - 1], y_r.at[p, d - 1], at_y(d),
        )

    def send_z(p, d):
        return remote(
            sent_z.at[(z + d) % NZ, p], got_z.at[d - 1, p],
            z_s.at[p, d - 1], z_r.at[p, d - 1], at_z(d),
        )

    def chip_sum(p, i):
        load(p, i).wait()
        swap(p, i).wait_recv()
        cy = (y + distance(i)) % NY
        cz = (cy + p) % 2
        for k in range(NX):
            rows = pl.ds(pl.multiple_of(((x + k) % NX) * 64, 64), 64)
            value = own[p, i, rows, :] + other[p, i, rows, :]
            sent_a[p, k, i] = value[:, :128].reshape(4, 16, 128)
            if k % 2 == 1:
                sent_y[cy, p, k // 2] = value[:, 128:].reshape(4, 16, 128)
            else:
                for hi in range(4):
                    sent_z[hi * 2 + cz, p, cy // 2, k // 2] = value[
                        hi * 16 : hi * 16 + 16, 128:
                    ]

    for p in range(2):

        def step(i):
            chip_sum(p, i)
            send_y(p, distance(i)).start()

        each(4, step)
        for k in range(1, NX):
            send_a(p, 0, k).start()
        if p == 0:
            for n in range(4):
                pl.semaphore_wait(far_sem.at[n], 1)
        each(7, step, first=4)
        chip_sum(p, 7)
        for k in range(1, NX):
            send_a(p, 1, k).start()
        each(7, lambda i: send_z(p, distance(i)).start())

    def send_a2(p, d):
        if p == 0:
            src, target = part_a.at[p, (y + d) % NY], at_y(d)
        else:
            src, target = part_a.at[p, (z + d) % NZ], at_z(d)
        return remote(
            src, got_a2.at[p, d - 1], a2_s.at[p, d - 1], a2_r.at[p, d - 1], target
        )

    def send_h2(way, d):
        if way == 0:
            src, target = part_h.at[way, (z + d) % NZ], at_z(d)
        else:
            src, target = part_h.at[way, (y + d) % NY], at_y(d)
        return remote(
            src, got_h2.at[way, d - 1], h2_s.at[way, d - 1], h2_r.at[way, d - 1], target
        )

    def start_h2(way, p):
        mine, crossing = (z, y) if way == 0 else (y, z)

        def step(n):
            d = (2 * n + (crossing + p) % 2 - mine + 8) % 8

            @pl.when(d != 0)
            def _():
                send_h2(way, d).start()

        each(4, step)

    def x_sum(p, i):
        value = sent_a[p, 0, i].astype(F32)
        for k in range(NX - 1):
            value += got_a[p, k, i].astype(F32)
        value = value.astype(BF16)
        cy = (y + distance(i)) % NY
        if p == 0:
            part_a[p, cy] = value
        else:
            for hi in range(4):
                part_a[p, hi * 2 + (cy + 1) % 2, cy // 2] = value[hi]

    def first_sums(p):
        for part in range(2):
            for k in range(1, NX):
                send_a(p, part, k).wait_recv()

            def step(i):
                x_sum(p, i)
                if p == 0:
                    send_a2(p, distance(i)).start()

            each(4 + 3 * part, step, first=4 * part)
            if part == 1:
                x_sum(p, 7)
        if p == 1:
            each(7, lambda i: send_a2(p, distance(6 - i)).start())

        each(NY - 1, lambda i: send_y(p, i + 1).wait_recv())
        for k in range(2):
            value = sent_y[y, p, k].astype(F32)
            for d in range(NY - 1):
                value += got_y[d, p, k].astype(F32)
            value = value.astype(BF16)
            for hi in range(4):
                part_h[0, hi * 2 + (y + p) % 2, k] = value[hi]
        start_h2(0, p)

        each(NZ - 1, lambda i: send_z(p, i + 1).wait_recv())

        def z_sum(ci):
            value = sent_z[z, p, ci].astype(F32)
            for d in range(NZ - 1):
                value += got_z[d, p, ci].astype(F32)
            part_h[1, 2 * ci + (z + p) % 2] = value.astype(BF16)

        each(4, z_sum)
        start_h2(1, p)

    def last_a(p, d):
        to_y = y if p == 0 else (y + d) % NY
        to_z = (z + d) % NZ if p == 0 else z
        index = (to_z if p == 0 else to_y) // 2
        return remote(
            sum_a.at[p, index], got_a3.at[d - 1],
            a3_s.at[d - 1], a3_r.at[d - 1], device(x, to_y, to_z, core),
        )

    def second_sum_a(p):
        each(NY - 1, lambda i: send_a2(p, i + 1).wait_recv())
        value = part_a[p, y if p == 0 else z].astype(F32)
        for d in range(NY - 1):
            value += got_a2[p, d].astype(F32)
        sum_a[p] = value.astype(BF16)

        def step(n):
            d = 2 * n + (odd + p) % 2

            @pl.when(d != 0)
            def _():
                last_a(p, d).start()

        each(4, step)

    def send_h3(k):
        return remote(
            sum_h.at[k], got_h3.at[k - 1], h3_s.at[k - 1], h3_r.at[k - 1], at_x(k)
        )

    first_sums(0)
    first_sums(1)
    second_sum_a(0)
    for way in range(2):
        each(NZ - 1, lambda i: send_h2(way, i + 1).wait_recv())
        value = part_h[way, z if way == 0 else y].astype(F32)
        for d in range(NZ - 1):
            value += got_h2[way, d].astype(F32)
        value = value.astype(BF16)
        for k in range(2):
            sum_h[2 * k + 1 - way] = value[k]
    for k in range(1, NX):
        send_h3(k).start()
    second_sum_a(1)

    for copy in states:
        copy.wait()

    def finish(half, total):
        cols = slice(half * 128, half * 128 + 128)
        new_master, new_first, new_second = adam(
            total, state[0, :, cols], state[1, :, cols], state[2, :, cols]
        )
        result[0, :, cols] = new_master
        result[1, :, cols] = new_first
        result[2, :, cols] = new_second
        weights[:, cols] = new_master.astype(BF16)

    for k in range(1, NX):
        send_h3(k).wait_recv()
    total = sum_h[0].astype(F32)
    for k in range(NX - 1):
        total += got_h3[k].astype(F32)
    finish(1, total)

    each(NY - 1, lambda i: last_a(0, i + 1).wait_recv())
    total = sum_a[odd, (z * (1 - odd) + y * odd) // 2].astype(F32)
    for d in range(NY - 1):
        total += got_a3[d].astype(F32)
    finish(0, total)

    rows = pl.ds(pl.multiple_of(outer * 16, 16), 16)

    def spread(n):
        return remote(
            weights, weights_out.at[rows], w_s.at[n - 1], w_r.at[n - 1],
            (inner, ((x + n // 4) % 4) * 4 + (z_hi + n % 4) % 4),
        )

    def arrive(n):
        source = ((x - n // 4 + 4) % 4) * 4 + (z_hi - n % 4 + 4) % 4
        return remote(
            weights, weights_out.at[pl.ds(pl.multiple_of(source * 16, 16), 16)],
            w_s.at[n - 1], w_r.at[n - 1], (inner, source),
        )

    for n in sorted(range(1, 16), key=lambda n: -hops(n)):
        spread(n).start()
    stores = [
        pltpu.make_async_copy(result, state_out, store_sem.at[0]),
        pltpu.make_async_copy(weights, weights_out.at[rows], store_sem.at[1]),
    ]
    for copy in stores:
        copy.start()

    for p in range(2):
        each(NY, lambda i: swap(p, i).wait_send())
        for k in range(1, NX):
            for part in range(2):
                send_a(p, part, k).wait_send()
        each(NY - 1, lambda i: send_y(p, i + 1).wait_send())
        each(NY - 1, lambda i: send_z(p, i + 1).wait_send())
        each(NY - 1, lambda i: send_a2(p, i + 1).wait_send())
        each(NY - 1, lambda i: send_h2(p, i + 1).wait_send())
    each(NY - 1, lambda i: last_a(0, i + 1).wait_send())
    for k in range(1, NX):
        send_h3(k).wait_send()
    for copy in stores:
        copy.wait()
    each(15, lambda i: spread(i + 1).wait_send())
    each(15, lambda i: arrive(i + 1).wait_recv())


def hand_out(state, weights, master_out, first_out, second_out, weights_out, held, block, sem):
    fetch = [
        pltpu.make_async_copy(state, held, sem.at[0]),
        pltpu.make_async_copy(weights, block, sem.at[1]),
    ]
    copies = [
        pltpu.make_async_copy(held.at[n], ref, sem.at[2 + n])
        for n, ref in enumerate((master_out, first_out, second_out))
    ] + [pltpu.make_async_copy(block, weights_out, sem.at[5])]
    for copy in fetch:
        copy.start()
    fetch[1].wait()
    copies[3].start()
    fetch[0].wait()
    for copy in copies[:3]:
        copy.start()
    for copy in copies:
        copy.wait()


def body(gradients, master_shard, first_moment, second_moment):
    grad = gradients.reshape(gradients.shape[2], gradients.shape[3])
    hbm = pl.BlockSpec(memory_space=pltpu.HBM)
    dma = pltpu.SemaphoreType.DMA
    shard = jax.ShapeDtypeStruct(master_shard.shape, F32)
    group = jax.ShapeDtypeStruct((256, 256), BF16)
    state, weights = pl.pallas_call(
        kernel,
        out_shape=(jax.ShapeDtypeStruct((3,) + master_shard.shape, F32), group),
        in_specs=[hbm] * 4,
        out_specs=(hbm,) * 2,
        scratch_shapes=[
            pltpu.VMEM((2, 8, 256, 256), BF16),
            pltpu.VMEM((2, 8, 256, 256), BF16),
            pltpu.VMEM((2, 4, 8, 4, 16, 128), BF16),
            pltpu.VMEM((2, 3, 8, 4, 16, 128), BF16),
            pltpu.VMEM((8, 2, 2, 4, 16, 128), BF16),
            pltpu.VMEM((7, 2, 2, 4, 16, 128), BF16),
            pltpu.VMEM((8, 2, 4, 2, 16, 128), BF16),
            pltpu.VMEM((7, 2, 4, 2, 16, 128), BF16),
            pltpu.VMEM((2, 8, 4, 16, 128), BF16),
            pltpu.VMEM((2, 7, 4, 16, 128), BF16),
            pltpu.VMEM((2, 4, 16, 128), BF16),
            pltpu.VMEM((7, 16, 128), BF16),
            pltpu.VMEM((2, 8, 2, 16, 128), BF16),
            pltpu.VMEM((2, 7, 2, 16, 128), BF16),
            pltpu.VMEM((4, 16, 128), BF16),
            pltpu.VMEM((3, 16, 128), BF16),
            pltpu.VMEM((3, 16, 256), F32),
            pltpu.VMEM((3, 16, 256), F32),
            pltpu.VMEM((16, 256), BF16),
            dma((2, 8)), dma((3,)), dma((2,)), pltpu.SemaphoreType.REGULAR((4,)),
            dma((2, 8)), dma((2, 8)),
            dma((2, 2, 3)), dma((2, 2, 3)),
            dma((2, 7)), dma((2, 7)),
            dma((2, 7)), dma((2, 7)),
            dma((2, 7)), dma((2, 7)),
            dma((2, 7)), dma((2, 7)),
            dma((7,)), dma((7,)),
            dma((3,)), dma((3,)),
            dma((15,)), dma((15,)),
        ],
        compiler_params=pltpu.CompilerParams(
            collective_id=0, has_side_effects=True, vmem_limit_bytes=60 << 20
        ),
        name="reduce_adam_gather",
    )(grad, master_shard, first_moment, second_moment)
    return pl.pallas_call(
        hand_out,
        out_shape=(shard, shard, shard, group),
        in_specs=[hbm] * 2,
        out_specs=(hbm,) * 4,
        scratch_shapes=[
            pltpu.VMEM((3,) + master_shard.shape, F32), pltpu.VMEM((256, 256), BF16), dma((6,)),
        ],
        compiler_params=pltpu.CompilerParams(vmem_limit_bytes=60 << 20),
        name="hand_out",
    )(state, weights)


def solution(mesh):
    return jax.shard_map(
        body,
        mesh=mesh,
        in_specs=(
            P("inner", "outer", None, None),
            P("outer", "inner"),
            P("outer", "inner"),
            P("outer", "inner"),
        ),
        out_specs=(P("outer", "inner"), P("outer", "inner"), P("outer", "inner"), P(None, "inner")),
        check_vma=False,
    )
```

time: 57.2 us -> 51.4 us (0.90)
  local copies, waits for them, and re-layouts: 5.54 us -> 0 us
    unnamed x4 -> x0, local copies, waits for them, and re-layouts: 5.54 us -> none
    pallas_call x1 -> x2, Pallas kernels: 50.6 us -> 50.6 us  [the longest x1 49 us: body(): pl.pallas_call(kernel, out_shape=(jax.ShapeDtypeStruct((3,) + master_shar...]
where the time goes in v2:
time: 51.4 us; the launch traced here: 51.2 us
  Pallas kernels  50.6 us (98%)
  between operations  0.64 us (1%)
    pallas_call x1, Pallas kernels, body(): pl.pallas_call(kernel, out_shape=(jax.ShapeDtypeStruct((3,) + master_shar...  49 us
    pallas_call x1, Pallas kernels, body(): pl.pallas_call(hand_out, out_shape=(shard, shard, shard, group), in_specs...  1.65 us

profile of v2, /device:TPU:8, one launch (start us, length us, event | category | flops | bytes accessed | tf_op | source)
XLA Modules:
  0.0 51.2 jit_solution(16148350719680139079)
XLA Ops:
  0.6 49.0 %reduce_adam_gather.1 = (f32[3,16,256]{2,1,0:T(8,128)}, bf16[256,256]{1,0:T(8,128)(2,1)}) custom-call(bf16[256,8192]{1,0:T(8,128)(2,1)} %bitcast.1, f32[16,256]{1,0:T(8,128)} %master_in.1, f32[16,256]{1,0:T(8,128)} %first_in.1, f32[16,256]{1,0:T(8,128)} %second_in.1), custom_call_target="tpu_custom_call" | custom-call | tf_op jit(solution)/shard_map/reduce_adam_gather/pallas_call | solution.py:403
  49.6 1.6 %hand_out.1 = (f32[16,256]{1,0:T(8,128)}, f32[16,256]{1,0:T(8,128)}, f32[16,256]{1,0:T(8,128)}, bf16[256,256]{1,0:T(8,128)(2,1)}) custom-call(f32[3,16,256]{2,1,0:T(8,128)} %get-tuple-element.6.state, bf16[256,256]{1,0:T(8,128)(2,1)} %get-tuple-element.7.weights), custom_call_target="tpu_custom_call" | custom-call | tf_op jit(solution)/shard_map/hand_out/pallas_call | solution.py:444

commit v3 on v2

--- a/solution.py
+++ b/solution.py
@@ -160,7 +160,7 @@
                 sent_y[cy, p, k // 2] = value[:, 128:].reshape(4, 16, 128)
             else:
                 for hi in range(4):
-                    sent_z[hi * 2 + cz, p, cy // 2, k // 2] = value[
+                    sent_z[hi * 2 + cz, p, cy // 2, 1 - k // 2] = value[
                         hi * 16 : hi * 16 + 16, 128:
                     ]
 
@@ -191,26 +191,11 @@
             src, got_a2.at[p, d - 1], a2_s.at[p, d - 1], a2_r.at[p, d - 1], target
         )
 
-    def send_h2(way, d):
-        if way == 0:
-            src, target = part_h.at[way, (z + d) % NZ], at_z(d)
-        else:
-            src, target = part_h.at[way, (y + d) % NY], at_y(d)
-        return remote(
-            src, got_h2.at[way, d - 1], h2_s.at[way, d - 1], h2_r.at[way, d - 1], target
-        )
-
-    def start_h2(way, p):
-        mine, crossing = (z, y) if way == 0 else (y, z)
-
-        def step(n):
-            d = (2 * n + (crossing + p) % 2 - mine + 8) % 8
-
-            @pl.when(d != 0)
-            def _():
-                send_h2(way, d).start()
-
-        each(4, step)
+    def send_h2(p, k):
+        return remote(
+            part_h.at[1 - k % 2, k // 2 if k % 2 else 0, p], got_h2.at[k - 1, p],
+            h2_s.at[p, k - 1], h2_r.at[p, k - 1], at_x(k),
+        )
 
     def x_sum(p, i):
         value = sent_a[p, 0, i].astype(F32)
@@ -246,9 +231,8 @@
             for d in range(NY - 1):
                 value += got_y[d, p, k].astype(F32)
             value = value.astype(BF16)
-            for hi in range(4):
-                part_h[0, hi * 2 + (y + p) % 2, k] = value[hi]
-        start_h2(0, p)
+            part_h[0, k, p] = value
+            send_h2(p, 2 * k + 1).start()
 
         each(NZ - 1, lambda i: send_z(p, i + 1).wait_recv())
 
@@ -256,10 +240,12 @@
             value = sent_z[z, p, ci].astype(F32)
             for d in range(NZ - 1):
                 value += got_z[d, p, ci].astype(F32)
-            part_h[1, 2 * ci + (z + p) % 2] = value.astype(BF16)
+            value = value.astype(BF16)
+            for k in range(2):
+                part_h[1, k, p, ci] = value[k]
 
         each(4, z_sum)
-        start_h2(1, p)
+        send_h2(p, 2).start()
 
     def last_a(p, d):
         to_y = y if p == 0 else (y + d) % NY
@@ -286,24 +272,36 @@
 
         each(4, step)
 
-    def send_h3(k):
-        return remote(
-            sum_h.at[k], got_h3.at[k - 1], h3_s.at[k - 1], h3_r.at[k - 1], at_x(k)
-        )
+    def last_h(way, d):
+        index = (z + d) % NZ if way == 0 else (y + d) % NY
+        return remote(
+            sum_h.at[way, index], got_h3.at[way, d - 1],
+            h3_s.at[way, d - 1], h3_r.at[way, d - 1], at_z(d) if way == 0 else at_y(d),
+        )
+
+    def second_sum_h(p):
+        for k in range(1, NX):
+            send_h2(p, k).wait_recv()
+        for way in range(2):
+            first = (got_h2[0, p] if way == 0 else part_h[1, 1, p]).astype(F32)
+            value = (first + got_h2[2 - way, p].astype(F32)).astype(BF16)
+            for n in range(4):
+                sum_h[way, 2 * n + ((y if way == 0 else z) + p) % 2] = value[n]
+
+            def step(n):
+                d = 2 * n + (odd + p) % 2
+
+                @pl.when(d != 0)
+                def _():
+                    last_h(way, d).start()
+
+            each(4, step)
 
     first_sums(0)
     first_sums(1)
     second_sum_a(0)
-    for way in range(2):
-        each(NZ - 1, lambda i: send_h2(way, i + 1).wait_recv())
-        value = part_h[way, z if way == 0 else y].astype(F32)
-        for d in range(NZ - 1):
-            value += got_h2[way, d].astype(F32)
-        value = value.astype(BF16)
-        for k in range(2):
-            sum_h[2 * k + 1 - way] = value[k]
-    for k in range(1, NX):
-        send_h3(k).start()
+    second_sum_h(0)
+    second_sum_h(1)
     second_sum_a(1)
 
     for copy in states:
@@ -319,11 +317,12 @@
         result[2, :, cols] = new_second
         weights[:, cols] = new_master.astype(BF16)
 
-    for k in range(1, NX):
-        send_h3(k).wait_recv()
-    total = sum_h[0].astype(F32)
-    for k in range(NX - 1):
-        total += got_h3[k].astype(F32)
+    for way in range(2):
+        each(NY - 1, lambda i: last_h(way, i + 1).wait_recv())
+    total = sum_h[0, z].astype(F32) + sum_h[1, y].astype(F32)
+    for way in range(2):
+        for d in range(NY - 1):
+            total += got_h3[way, d].astype(F32)
     finish(1, total)
 
     each(NY - 1, lambda i: last_a(0, i + 1).wait_recv())
@@ -364,10 +363,10 @@
         each(NY - 1, lambda i: send_y(p, i + 1).wait_send())
         each(NY - 1, lambda i: send_z(p, i + 1).wait_send())
         each(NY - 1, lambda i: send_a2(p, i + 1).wait_send())
-        each(NY - 1, lambda i: send_h2(p, i + 1).wait_send())
+        for k in range(1, NX):
+            send_h2(p, k).wait_send()
+        each(NY - 1, lambda i: last_h(p, i + 1).wait_send())
     each(NY - 1, lambda i: last_a(0, i + 1).wait_send())
-    for k in range(1, NX):
-        send_h3(k).wait_send()
     for copy in stores:
         copy.wait()
     each(15, lambda i: spread(i + 1).wait_send())
@@ -418,10 +417,10 @@
             pltpu.VMEM((2, 7, 4, 16, 128), BF16),
             pltpu.VMEM((2, 4, 16, 128), BF16),
             pltpu.VMEM((7, 16, 128), BF16),
-            pltpu.VMEM((2, 8, 2, 16, 128), BF16),
-            pltpu.VMEM((2, 7, 2, 16, 128), BF16),
-            pltpu.VMEM((4, 16, 128), BF16),
-            pltpu.VMEM((3, 16, 128), BF16),
+            pltpu.VMEM((2, 2, 2, 4, 16, 128), BF16),
+            pltpu.VMEM((3, 2, 4, 16, 128), BF16),
+            pltpu.VMEM((2, 8, 16, 128), BF16),
+            pltpu.VMEM((2, 7, 16, 128), BF16),
             pltpu.VMEM((3, 16, 256), F32),
             pltpu.VMEM((3, 16, 256), F32),
             pltpu.VMEM((16, 256), BF16),
@@ -431,9 +430,9 @@
             dma((2, 7)), dma((2, 7)),
             dma((2, 7)), dma((2, 7)),
             dma((2, 7)), dma((2, 7)),
+            dma((2, 3)), dma((2, 3)),
+            dma((7,)), dma((7,)),
             dma((2, 7)), dma((2, 7)),
-            dma((7,)), dma((7,)),
-            dma((3,)), dma((3,)),
             dma((15,)), dma((15,)),
         ],
         compiler_params=pltpu.CompilerParams(

time: 51.4 us -> 49.8 us (0.969)
  Pallas kernels: 50.6 us -> 48.9 us
    pallas_call x1, Pallas kernels: 49 us -> 47.2 us  [body(): pl.pallas_call(kernel, out_shape=(jax.ShapeDtypeStruct((3,) + master_shar...]
where the time goes in v3:
time: 49.8 us; the launch traced here: 49.5 us
  Pallas kernels  48.9 us (98%)
  between operations  0.64 us (1%)
    pallas_call x1, Pallas kernels, body(): pl.pallas_call(kernel, out_shape=(jax.ShapeDtypeStruct((3,) + master_shar...  47.2 us
    pallas_call x1, Pallas kernels, body(): pl.pallas_call(hand_out, out_shape=(shard, shard, shard, group), in_specs...  1.65 us

profile of v3, /device:TPU:8, one launch (start us, length us, event | category | flops | bytes accessed | tf_op | source)
XLA Modules:
  0.0 49.5 jit_solution(18135030651290567336)
XLA Ops:
  0.6 47.2 %reduce_adam_gather.1 = (f32[3,16,256]{2,1,0:T(8,128)}, bf16[256,256]{1,0:T(8,128)(2,1)}) custom-call(bf16[256,8192]{1,0:T(8,128)(2,1)} %bitcast.1, f32[16,256]{1,0:T(8,128)} %master_in.1, f32[16,256]{1,0:T(8,128)} %first_in.1, f32[16,256]{1,0:T(8,128)} %second_in.1), custom_call_target="tpu_custom_call" | custom-call | tf_op jit(solution)/shard_map/reduce_adam_gather/pallas_call | solution.py:402
  47.9 1.6 %hand_out.1 = (f32[16,256]{1,0:T(8,128)}, f32[16,256]{1,0:T(8,128)}, f32[16,256]{1,0:T(8,128)}, bf16[256,256]{1,0:T(8,128)(2,1)}) custom-call(f32[3,16,256]{2,1,0:T(8,128)} %get-tuple-element.6.state, bf16[256,256]{1,0:T(8,128)(2,1)} %get-tuple-element.7.weights), custom_call_target="tpu_custom_call" | custom-call | tf_op jit(solution)/shard_map/hand_out/pallas_call | solution.py:443

commit v4 on v3

v4 whole, which is shorter than its diff:
```python
import jax
import jax.numpy as jnp
from jax import lax
from jax.experimental import pallas as pl
from jax.experimental.pallas import tpu as pltpu
from jax.sharding import PartitionSpec as P

MESH = pl.DeviceIdType.MESH
F32 = jnp.float32
BF16 = jnp.bfloat16

beta_first = 0.9
beta_second = 0.95
learn_rate = 0.05
decay_rate = 0.1
adam_eps = 1e-05
bias_first = 1.0 - 0.9**10
bias_second = 1.0 - 0.95**10

NX, NY, NZ = 4, 8, 8


def mod(value, n):
    return value % n if isinstance(value, int) else lax.rem(value, jnp.int32(n))


def div(value, n):
    return value // n if isinstance(value, int) else lax.div(value, jnp.int32(n))


def adam(total, master, first, second):
    new_first = beta_first * first + (1.0 - beta_first) * total
    new_second = beta_second * second + (1.0 - beta_second) * total * total
    update = (
        new_first / bias_first / (jnp.sqrt(new_second / bias_second) + adam_eps)
        + decay_rate * master
    )
    return master - learn_rate * update, new_first, new_second


def each(count, step, first=0):
    def body(i, carry):
        step(i)
        return carry

    lax.fori_loop(first, count, body, 0)


def distance(i):
    return mod((div(i, 2) + 1) * (1 - 2 * mod(i, 2)) + 8, 8) * (1 - div(i, 7))


FAR_FIRST = (4, 3, 5, 2, 6, 1, 7)


def hops(n):
    return min(n // 4, 4 - n // 4) + 2 * min(n % 4, 4 - n % 4)


def kernel(
    grad, master_in, first_in, second_in,
    state_out, weights_out,
    own, other, sent_a, got_a, sent_y, got_y, sent_z, got_z,
    part_a, got_a2, sum_a, got_a3, part_h, got_h2, sum_h, got_h3,
    state, result, weights,
    load_sem, state_sem, store_sem, far_sem,
    core_s, core_r, a_s, a_r, y_s, y_r, z_s, z_r,
    a2_s, a2_r, h2_s, h2_r, a3_s, a3_r, h3_s, h3_r, w_s, w_r,
):
    inner = lax.axis_index("inner")
    outer = lax.axis_index("outer")
    core = mod(inner, 2)
    y = mod(div(inner, 2), NY)
    z_lo = div(inner, 16)
    x = div(outer, 4)
    z_hi = mod(outer, 4)
    z = z_hi * 2 + z_lo
    odd = mod(y + z, 2)

    def at_x(d):
        return (inner, mod(x + d, NX) * 4 + z_hi)

    def at_y(d):
        return (z_lo * 16 + mod(y + d, NY) * 2 + core, outer)

    def at_z(d):
        other_z = mod(z + d, NZ)
        return (mod(other_z, 2) * 16 + y * 2 + core, x * 4 + div(other_z, 2))

    sibling = (inner + 1 - 2 * core, outer)

    def arrived(ref, sem):
        pltpu.make_async_copy(ref, ref, sem).wait()

    def remote(src, dst, send, recv, target):
        return pltpu.make_async_remote_copy(
            src_ref=src, dst_ref=dst, send_sem=send, recv_sem=recv,
            device_id=target, device_id_type=MESH,
        )

    barrier = pltpu.get_barrier_semaphore()
    near = (
        [at_x(d) for d in (2, 1, 3)]
        + [at_y(d) for d in (2, 6, 1, 7)]
        + [at_z(d) for d in (2, 6, 1, 7)]
        + [sibling]
    )
    for peer in near:
        pl.semaphore_signal(barrier, inc=1, device_id=peer, device_id_type=MESH)

    def column(p, i, which):
        cy = mod(y + distance(i), NY)
        start = (mod(cy + p, 2) * 16 + cy * 2 + which) * 256
        return pl.ds(pl.multiple_of(start, 256), 256)

    def load(p, i):
        return pltpu.make_async_copy(
            grad.at[:, column(p, i, core)], own.at[p, i], load_sem.at[p, i]
        )

    def swap(p, i):
        return remote(
            grad.at[:, column(p, i, 1 - core)], other.at[p, i],
            core_s.at[0], core_r.at[p, i], sibling,
        )

    for p in range(2):
        each(NY, lambda i: load(p, i).start())
    states = [
        pltpu.make_async_copy(ref, state.at[n], state_sem.at[n])
        for n, ref in enumerate((master_in, first_in, second_in))
    ]
    for copy in states:
        copy.start()

    pl.semaphore_wait(barrier, len(near))
    two_away = (at_y(2), at_y(6), at_z(2), at_z(6))
    for n, peer in enumerate(two_away):
        pl.semaphore_signal(far_sem.at[n], inc=1, device_id=peer, device_id_type=MESH)
    for p in range(2):
        each(NY, lambda i: swap(p, i).start())

    def send_a(p, part, k):
        blocks = pl.ds(part * 4, 4)
        return remote(
            sent_a.at[p, k, blocks], got_a.at[p, k - 1, blocks],
            a_s.at[0], a_r.at[p, part], at_x(k),
        )

    def send_y(p, d):
        return remote(
            sent_y.at[mod(y + d, NY), p], got_y.at[d - 1, p],
            y_s.at[0], y_r.at[p], at_y(d),
        )

    def send_z(p, d):
        return remote(
            sent_z.at[mod(z + d, NZ), p], got_z.at[d - 1, p],
            z_s.at[0], z_r.at[p], at_z(d),
        )

    def chip_sum(p, i):
        load(p, i).wait()
        swap(p, i).wait_recv()
        cy = mod(y + distance(i), NY)
        cz = mod(cy + p, 2)
        for k in range(NX):
            rows = pl.ds(pl.multiple_of(mod(x + k, NX) * 64, 64), 64)
            value = own[p, i, rows, :] + other[p, i, rows, :]
            sent_a[p, k, i] = value[:, :128].reshape(4, 16, 128)
            if k % 2 == 1:
                sent_y[cy, p, k // 2] = value[:, 128:].reshape(4, 16, 128)
            else:
                for hi in range(4):
                    sent_z[hi * 2 + cz, p, div(cy, 2), 1 - k // 2] = value[
                        hi * 16 : hi * 16 + 16, 128:
                    ]

    for p in range(2):

        def step(i):
            chip_sum(p, i)
            send_y(p, distance(i)).start()

        each(4, step)
        for k in range(1, NX):
            send_a(p, 0, k).start()
        if p == 0:
            for n in range(4):
                pl.semaphore_wait(far_sem.at[n], 1)
        each(7, step, first=4)
        chip_sum(p, 7)
        for k in range(1, NX):
            send_a(p, 1, k).start()
        for d in FAR_FIRST:
            send_z(p, d).start()

    def send_a2(p, d):
        if p == 0:
            src, target = part_a.at[p, mod(y + d, NY)], at_y(d)
        else:
            src, target = part_a.at[p, mod(z + d, NZ)], at_z(d)
        return remote(
            src, got_a2.at[p, d - 1], a2_s.at[0], a2_r.at[p], target
        )

    def send_h2(p, k):
        return remote(
            part_h.at[1 - k % 2, k // 2 if k % 2 else 0, p], got_h2.at[k - 1, p],
            h2_s.at[0], h2_r.at[p], at_x(k),
        )

    def x_sum(p, i):
        value = sent_a[p, 0, i].astype(F32)
        for k in range(NX - 1):
            value += got_a[p, k, i].astype(F32)
        value = value.astype(BF16)
        cy = mod(y + distance(i), NY)
        if p == 0:
            part_a[p, cy] = value
        else:
            for hi in range(4):
                part_a[p, hi * 2 + mod(cy + 1, 2), div(cy, 2)] = value[hi]

    def first_sums(p):
        for part in range(2):
            arrived(got_a.at[p, :, pl.ds(4 * part, 4)], a_r.at[p, part])
            each(4 + 4 * part, lambda i: x_sum(p, i), first=4 * part)
        for d in FAR_FIRST:
            send_a2(p, d).start()

        arrived(got_y.at[:, p], y_r.at[p])
        for k in range(2):
            value = sent_y[y, p, k].astype(F32)
            for d in range(NY - 1):
                value += got_y[d, p, k].astype(F32)
            value = value.astype(BF16)
            part_h[0, k, p] = value
            send_h2(p, 2 * k + 1).start()

        arrived(got_z.at[:, p], z_r.at[p])

        def z_sum(ci):
            value = sent_z[z, p, ci].astype(F32)
            for d in range(NZ - 1):
                value += got_z[d, p, ci].astype(F32)
            value = value.astype(BF16)
            for k in range(2):
                part_h[1, k, p, ci] = value[k]

        each(4, z_sum)
        send_h2(p, 2).start()

    def last_a(p, d):
        to_y = y if p == 0 else mod(y + d, NY)
        to_z = mod(z + d, NZ) if p == 0 else z
        index = div(to_z if p == 0 else to_y, 2)
        return remote(
            sum_a.at[p, index], got_a3.at[d - 1],
            a3_s.at[0], a3_r.at[0], at_z(d) if p == 0 else at_y(d),
        )

    def to_owners(p, act):
        shift = mod(odd + p, 2)
        for n in (2, 1, 3):
            act(2 * n + shift)

        @pl.when(shift != 0)
        def _():
            act(shift)

    def second_sum_a(p):
        arrived(got_a2.at[p], a2_r.at[p])
        value = part_a[p, y if p == 0 else z].astype(F32)
        for d in range(NY - 1):
            value += got_a2[p, d].astype(F32)
        sum_a[p] = value.astype(BF16)

        to_owners(p, lambda d: last_a(p, d).start())

    def last_h(way, d):
        index = mod(z + d, NZ) if way == 0 else mod(y + d, NY)
        return remote(
            sum_h.at[way, index], got_h3.at[way, d - 1],
            h3_s.at[0], h3_r.at[way], at_z(d) if way == 0 else at_y(d),
        )

    def second_sum_h(p):
        arrived(got_h2.at[:, p], h2_r.at[p])
        for way in range(2):
            first = (got_h2[0, p] if way == 0 else part_h[1, 1, p]).astype(F32)
            value = (first + got_h2[2 - way, p].astype(F32)).astype(BF16)
            for n in range(4):
                sum_h[way, 2 * n + mod((y if way == 0 else z) + p, 2)] = value[n]

            to_owners(p, lambda d: last_h(way, d).start())

    first_sums(0)
    first_sums(1)
    second_sum_a(0)
    second_sum_h(0)
    second_sum_h(1)
    second_sum_a(1)

    for copy in states:
        copy.wait()

    def finish(half, total):
        cols = slice(half * 128, half * 128 + 128)
        new_master, new_first, new_second = adam(
            total, state[0, :, cols], state[1, :, cols], state[2, :, cols]
        )
        result[0, :, cols] = new_master
        result[1, :, cols] = new_first
        result[2, :, cols] = new_second
        weights[:, cols] = new_master.astype(BF16)

    for way in range(2):
        arrived(got_h3.at[way], h3_r.at[way])
    total = sum_h[0, z].astype(F32) + sum_h[1, y].astype(F32)
    for way in range(2):
        for d in range(NY - 1):
            total += got_h3[way, d].astype(F32)
    finish(1, total)

    arrived(got_a3, a3_r.at[0])
    total = sum_a[odd, div(z * (1 - odd) + y * odd, 2)].astype(F32)
    for d in range(NY - 1):
        total += got_a3[d].astype(F32)
    finish(0, total)

    rows = pl.ds(pl.multiple_of(outer * 16, 16), 16)

    def spread(n):
        return remote(
            weights, weights_out.at[rows], w_s.at[0], w_r.at[0],
            (inner, mod(x + n // 4, 4) * 4 + mod(z_hi + n % 4, 4)),
        )

    for n in sorted(range(1, 16), key=lambda n: -hops(n)):
        spread(n).start()
    stores = [
        pltpu.make_async_copy(result, state_out, store_sem.at[0]),
        pltpu.make_async_copy(weights, weights_out.at[rows], store_sem.at[1]),
    ]
    for copy in stores:
        copy.start()

    for ref, sem in (
        (other, core_s), (sent_a.at[:, pl.ds(1, 3)], a_s), (got_y, y_s), (got_z, z_s),
        (got_a2, a2_s), (got_h2, h2_s), (got_a3, a3_s), (got_h3, h3_s),
        (weights_out.at[pl.ds(0, 240)], w_s),
    ):
        arrived(ref, sem.at[0])
    for copy in stores:
        copy.wait()
    arrived(weights_out.at[pl.ds(0, 240)], w_r.at[0])


def hand_out(state, weights, master_out, first_out, second_out, weights_out, sem):
    copies = [
        pltpu.make_async_copy(state.at[n], ref, sem.at[n])
        for n, ref in enumerate((master_out, first_out, second_out))
    ] + [pltpu.make_async_copy(weights, weights_out, sem.at[3])]
    for copy in copies:
        copy.start()
    for copy in copies:
        copy.wait()


def body(gradients, master_shard, first_moment, second_moment):
    grad = gradients.reshape(gradients.shape[2], gradients.shape[3])
    hbm = pl.BlockSpec(memory_space=pltpu.HBM)
    dma = pltpu.SemaphoreType.DMA
    shard = jax.ShapeDtypeStruct(master_shard.shape, F32)
    group = jax.ShapeDtypeStruct((256, 256), BF16)
    state, weights = pl.pallas_call(
        kernel,
        out_shape=(jax.ShapeDtypeStruct((3,) + master_shard.shape, F32), group),
        in_specs=[hbm] * 4,
        out_specs=(hbm,) * 2,
        scratch_shapes=[
            pltpu.VMEM((2, 8, 256, 256), BF16),
            pltpu.VMEM((2, 8, 256, 256), BF16),
            pltpu.VMEM((2, 4, 8, 4, 16, 128), BF16),
            pltpu.VMEM((2, 3, 8, 4, 16, 128), BF16),
            pltpu.VMEM((8, 2, 2, 4, 16, 128), BF16),
            pltpu.VMEM((7, 2, 2, 4, 16, 128), BF16),
            pltpu.VMEM((8, 2, 4, 2, 16, 128), BF16),
            pltpu.VMEM((7, 2, 4, 2, 16, 128), BF16),
            pltpu.VMEM((2, 8, 4, 16, 128), BF16),
            pltpu.VMEM((2, 7, 4, 16, 128), BF16),
            pltpu.VMEM((2, 4, 16, 128), BF16),
            pltpu.VMEM((7, 16, 128), BF16),
            pltpu.VMEM((2, 2, 2, 4, 16, 128), BF16),
            pltpu.VMEM((3, 2, 4, 16, 128), BF16),
            pltpu.VMEM((2, 8, 16, 128), BF16),
            pltpu.VMEM((2, 7, 16, 128), BF16),
            pltpu.VMEM((3, 16, 256), F32),
            pltpu.VMEM((3, 16, 256), F32),
            pltpu.VMEM((16, 256), BF16),
            dma((2, 8)), dma((3,)), dma((2,)), pltpu.SemaphoreType.REGULAR((4,)),
            dma((1,)), dma((2, 8)),
            dma((1,)), dma((2, 2)),
            dma((1,)), dma((2,)),
            dma((1,)), dma((2,)),
            dma((1,)), dma((2,)),
            dma((1,)), dma((2,)),
            dma((1,)), dma((1,)),
            dma((1,)), dma((2,)),
            dma((1,)), dma((1,)),
        ],
        compiler_params=pltpu.CompilerParams(
            collective_id=0, has_side_effects=True, vmem_limit_bytes=52 << 20
        ),
        name="reduce_adam_gather",
    )(*[pltpu.with_memory_space_constraint(v, pltpu.HBM) for v in (grad, master_shard, first_moment, second_moment)])
    return pl.pallas_call(
        hand_out,
        out_shape=(shard, shard, shard, group),
        in_specs=[hbm] * 2,
        out_specs=(hbm,) * 4,
        scratch_shapes=[dma((4,))],
        compiler_params=pltpu.CompilerParams(vmem_limit_bytes=52 << 20),
        name="hand_out",
    )(state, weights)


def solution(mesh):
    return jax.shard_map(
        body,
        mesh=mesh,
        in_specs=(
            P("inner", "outer", None, None),
            P("outer", "inner"),
            P("outer", "inner"),
            P("outer", "inner"),
        ),
        out_specs=(P("outer", "inner"), P("outer", "inner"), P("outer", "inner"), P(None, "inner")),
        check_vma=False,
    )
```

time: 49.8 us -> 46.6 us (0.936)
  Pallas kernels: 48.9 us -> 45.8 us
    pallas_call x1, Pallas kernels: 47.2 us -> 45.1 us  [body(): pl.pallas_call(kernel, out_shape=(jax.ShapeDtypeStruct((3,) + master_shar...]
    pallas_call x1, Pallas kernels: 1.65 us -> 0.71 us  [body(): pl.pallas_call(hand_out, out_shape=(shard, shard, shard, group), in_specs...]
where the time goes in v4:
time: 46.6 us; the launch traced here: 46.5 us
  Pallas kernels  45.8 us (98%)
  between operations  0.64 us (1%)
    pallas_call x1, Pallas kernels, body(): pl.pallas_call(kernel, out_shape=(jax.ShapeDtypeStruct((3,) + master_shar...  45.1 us

profile of v4, /device:TPU:8, one launch (start us, length us, event | category | flops | bytes accessed | tf_op | source)
XLA Modules:
  0.0 46.5 jit_solution(2401529346812909566)
XLA Ops:
  0.6 45.1 %reduce_adam_gather.1 = (f32[3,16,256]{2,1,0:T(8,128)S(1)}, bf16[256,256]{1,0:T(8,128)(2,1)S(1)}) custom-call(bf16[256,8192]{1,0:T(8,128)(2,1)} %bitcast.1, f32[16,256]{1,0:T(8,128)} %master_in.1, f32[16,256]{1,0:T(8,128)} %first_in.1, f32[16,256]{1,0:T(8,128)} %second_in.1), custom_call_target="tpu_custom_call" | custom-call | tf_op jit(solution)/shard_map/reduce_adam_gather/pallas_call | solution.py:377
  45.8 0.7 %hand_out.1 = (f32[16,256]{1,0:T(8,128)}, f32[16,256]{1,0:T(8,128)}, f32[16,256]{1,0:T(8,128)}, bf16[256,256]{1,0:T(8,128)(2,1)}) custom-call(f32[3,16,256]{2,1,0:T(8,128)S(1)} %get-tuple-element.6.state, bf16[256,256]{1,0:T(8,128)(2,1)S(1)} %get-tuple-element.7.weights), custom_call_target="tpu_custom_call" | custom-call | tf_op jit(solution)/shard_map/hand_out/pallas_call | solution.py:418

commit v5 on v4

--- a/solution.py
+++ b/solution.py
@@ -63,7 +63,7 @@
     own, other, sent_a, got_a, sent_y, got_y, sent_z, got_z,
     part_a, got_a2, sum_a, got_a3, part_h, got_h2, sum_h, got_h3,
     state, result, weights,
-    load_sem, state_sem, store_sem, far_sem,
+    load_sem, state_sem, store_sem, far_sem, x_r,
     core_s, core_r, a_s, a_r, y_s, y_r, z_s, z_r,
     a2_s, a2_r, h2_s, h2_r, a3_s, a3_r, h3_s, h3_r, w_s, w_r,
 ):
@@ -140,12 +140,24 @@
     for p in range(2):
         each(NY, lambda i: swap(p, i).start())
 
-    def send_a(p, part, k):
-        blocks = pl.ds(part * 4, 4)
-        return remote(
-            sent_a.at[p, k, blocks], got_a.at[p, k - 1, blocks],
-            a_s.at[0], a_r.at[p, part], at_x(k),
-        )
+    def pass_x(p, way, n):
+        k = 2 if n == 0 else 1 + 2 * way
+        blocks = pl.ds(4 * (way if n != 1 else 1 - way), 4)
+        return remote(
+            sent_a.at[p, k, blocks], got_a.at[p, min(n, 1), way, max(n - 1, 0)],
+            a_s.at[0], a_r.at[p, min(n, 1)] if n else x_r.at[p, way], at_x(1 + 2 * way),
+        )
+
+    def start_x(p, part):
+        pass_x(p, part, 0).start()
+        pass_x(p, 1 - part, 1).start()
+
+    def forward_x(p):
+        for way in range(2):
+            pass_x(p, way, 0).wait_recv()
+            for i in range(4):
+                sent_a[p, 1 + 2 * way, 4 * way + i] += got_a[p, 0, way, 0, i]
+            pass_x(p, way, 2).start()
 
     def send_y(p, d):
         return remote(
@@ -183,17 +195,19 @@
             send_y(p, distance(i)).start()
 
         each(4, step)
-        for k in range(1, NX):
-            send_a(p, 0, k).start()
+        start_x(p, 0)
         if p == 0:
             for n in range(4):
                 pl.semaphore_wait(far_sem.at[n], 1)
         each(7, step, first=4)
         chip_sum(p, 7)
-        for k in range(1, NX):
-            send_a(p, 1, k).start()
+        start_x(p, 1)
+        if p == 1:
+            forward_x(0)
         for d in FAR_FIRST:
             send_z(p, d).start()
+
+    forward_x(1)
 
     def send_a2(p, d):
         if p == 0:
@@ -210,10 +224,10 @@
             h2_s.at[0], h2_r.at[p], at_x(k),
         )
 
-    def x_sum(p, i):
+    def x_sum(p, i, part):
         value = sent_a[p, 0, i].astype(F32)
-        for k in range(NX - 1):
-            value += got_a[p, k, i].astype(F32)
+        for way in range(2):
+            value += got_a[p, 1, way, 1 if way == part else 0, i - 4 * part].astype(F32)
         value = value.astype(BF16)
         cy = mod(y + distance(i), NY)
         if p == 0:
@@ -223,9 +237,9 @@
                 part_a[p, hi * 2 + mod(cy + 1, 2), div(cy, 2)] = value[hi]
 
     def first_sums(p):
+        arrived(got_a.at[p, 1], a_r.at[p, 1])
         for part in range(2):
-            arrived(got_a.at[p, :, pl.ds(4 * part, 4)], a_r.at[p, part])
-            each(4 + 4 * part, lambda i: x_sum(p, i), first=4 * part)
+            each(4 + 4 * part, lambda i: x_sum(p, i, part), first=4 * part)
         for d in FAR_FIRST:
             send_a2(p, d).start()
 
@@ -383,7 +397,7 @@
             pltpu.VMEM((2, 8, 256, 256), BF16),
             pltpu.VMEM((2, 8, 256, 256), BF16),
             pltpu.VMEM((2, 4, 8, 4, 16, 128), BF16),
-            pltpu.VMEM((2, 3, 8, 4, 16, 128), BF16),
+            pltpu.VMEM((2, 2, 2, 2, 4, 4, 16, 128), BF16),
             pltpu.VMEM((8, 2, 2, 4, 16, 128), BF16),
             pltpu.VMEM((7, 2, 2, 4, 16, 128), BF16),
             pltpu.VMEM((8, 2, 4, 2, 16, 128), BF16),
@@ -399,7 +413,7 @@
             pltpu.VMEM((3, 16, 256), F32),
             pltpu.VMEM((3, 16, 256), F32),
             pltpu.VMEM((16, 256), BF16),
-            dma((2, 8)), dma((3,)), dma((2,)), pltpu.SemaphoreType.REGULAR((4,)),
+            dma((2, 8)), dma((3,)), dma((2,)), pltpu.SemaphoreType.REGULAR((4,)), dma((2, 2)),
             dma((1,)), dma((2, 8)),
             dma((1,)), dma((2, 2)),
             dma((1,)), dma((2,)),

time: 46.6 us -> 46 us (0.987)
  Pallas kernels: 45.8 us -> 45.3 us
    pallas_call x1, Pallas kernels: 45.1 us -> 44.6 us  [body(): pl.pallas_call(kernel, out_shape=(jax.ShapeDtypeStruct((3,) + master_shar...]
where the time goes in v5:
time: 46 us; the launch traced here: 45.9 us
  Pallas kernels  45.3 us (98%)
  between operations  0.64 us (1%)
    pallas_call x1, Pallas kernels, body(): pl.pallas_call(kernel, out_shape=(jax.ShapeDtypeStruct((3,) + master_shar...  44.6 us

profile of v5, /device:TPU:8, one launch (start us, length us, event | category | flops | bytes accessed | tf_op | source)
XLA Modules:
  0.0 45.9 jit_solution(13218374284243736177)
XLA Ops:
  0.6 44.6 %reduce_adam_gather.1 = (f32[3,16,256]{2,1,0:T(8,128)S(1)}, bf16[256,256]{1,0:T(8,128)(2,1)S(1)}) custom-call(bf16[256,8192]{1,0:T(8,128)(2,1)} %bitcast.1, f32[16,256]{1,0:T(8,128)} %master_in.1, f32[16,256]{1,0:T(8,128)} %first_in.1, f32[16,256]{1,0:T(8,128)} %second_in.1), custom_call_target="tpu_custom_call" | custom-call | tf_op jit(solution)/shard_map/reduce_adam_gather/pallas_call | solution.py:391
  45.2 0.7 %hand_out.1 = (f32[16,256]{1,0:T(8,128)}, f32[16,256]{1,0:T(8,128)}, f32[16,256]{1,0:T(8,128)}, bf16[256,256]{1,0:T(8,128)(2,1)}) custom-call(f32[3,16,256]{2,1,0:T(8,128)S(1)} %get-tuple-element.6.state, bf16[256,256]{1,0:T(8,128)(2,1)S(1)} %get-tuple-element.7.weights), custom_call_target="tpu_custom_call" | custom-call | tf_op jit(solution)/shard_map/hand_out/pallas_call | solution.py:432
